TPU v7x, 32 devices: a whole 2x2x4 slice. The times are simulated.
32 devices in a mesh: groups: 2 (over x), head: 8 (over z, y), tensor: 2 (over core).
Axes of the slice: x: 2, y: 2, z: 4, core: 2. Of those that a mesh axis runs over, the one named last changes fastest.
Arguments:
- query: bfloat16 [8192, 1024], P(('groups', 'head'), 'tensor'), parts along dimension 0, may hold values from -32 to 32
- keys_in: bfloat16 [8192, 1024], P(('groups', 'head'), 'tensor'), parts along dimension 0, may hold values from -6 to 6
- values_in: bfloat16 [8192, 1024], P(('groups', 'head'), 'tensor'), parts along dimension 0, may hold values from -6 to 6
- grad_out: bfloat16 [8192, 1024], P(('groups', 'head'), 'tensor'), parts along dimension 0, may hold values from -96 to 96
- w_out: bfloat16 [1024, 1024], P('tensor'), may hold values from -0.1875 to 0.1875
- w_query: bfloat16 [1024, 1024], P(None, 'tensor'), may hold values from -0.1875 to 0.1875
- w_key: bfloat16 [1024, 1024], P(None, 'tensor'), may hold values from -0.1875 to 0.1875
- w_value: bfloat16 [1024, 1024], P(None, 'tensor'), may hold values from -0.1875 to 0.1875
- perm: int32 [2, 4096], P('groups'), parts along dimension 0, may hold values from 0 to 4095, as said below
- blocks: int32 [2, 32, 12], P('groups'), parts along dimension 0, may hold values from 0 to 31, as said below
- counts: int32 [2, 32], P('groups'), parts along dimension 0, may hold values from 1 to 12
Outputs:
- input_grad: bfloat16 [8192, 1024], P(('groups', 'head', 'tensor')), parts along dimension 0
There are 2 independent parts, one for each index of `groups`. A program takes and returns all parts, laid end to end along the dimension named above; an argument that names none is the same for every part. Nothing has to cross between parts.
Inputs may be any that keep to these rules, and one draw needn't show every extreme that they name: Each row of perm holds every node number of the graph once. blocks[g, b, 0] is b; the 12 entries of blocks[g, b] are different block numbers.
All inputs are finite; a program needn't handle non-finite values.
Results may differ from a plain program's by a relative error of at most 0.011.
Values may be sent and summed in bfloat16 or wider, within the bound.
A program may use at most 64 MiB of HBM per device.

v0:
```python
import jax
import jax.numpy as jnp
from jax import lax
from jax.sharding import PartitionSpec as P

HD = 64
BS = 128
KB = 12


def on_device(
    query, keys_in, values_in, grad_out, w_out, w_query, w_key, w_value, perm, blocks, counts
):
    local_rows, half_width = query.shape
    graph_count, graph_nodes = perm.shape
    half_heads = half_width // HD
    part_rows = local_rows // graph_count
    block_count = graph_nodes // BS
    group_size = 512 // BS
    scale = HD ** (-0.5)
    attn_grad = lax.dot_general(
        lax.all_gather(grad_out, "tensor", axis=1, tiled=True),
        w_out,
        (((1,), (1,)), ((), ())),
        preferred_element_type=jnp.float32,
    ).astype(jnp.bfloat16)
    shaped = [
        member.reshape(part_rows, graph_count * half_heads, HD)
        for member in (query, keys_in, values_in, attn_grad)
    ]
    packed = jnp.stack(shaped, axis=2).reshape(part_rows, graph_count * half_heads, 4 * HD)
    arrived = lax.all_to_all(packed, "head", split_axis=1, concat_axis=0, tiled=True).reshape(
        graph_nodes, 4, HD
    )
    position = lax.axis_index("head")
    graph = position // half_heads
    order = lax.dynamic_index_in_dim(perm, graph, 0, keepdims=False)
    inverse = (
        jnp.zeros((graph_nodes,), jnp.int32).at[order].set(jnp.arange(graph_nodes, dtype=jnp.int32))
    )
    by_node = jnp.take(arrived, inverse, axis=0).reshape(block_count, BS, 4, HD)
    query_blk = by_node[:, :, 0]
    keyval = by_node[:, :, 1:3].reshape(block_count, BS, 2 * HD)
    grad_blk = by_node[:, :, 3]
    block_row = lax.dynamic_index_in_dim(blocks, graph, 0, keepdims=False)
    count_row = lax.dynamic_index_in_dim(counts, graph, 0, keepdims=False)
    live = jnp.arange(KB, dtype=jnp.int32)[None, :] < count_row[:, None]

    def one_group(carry, first):
        queries = lax.dynamic_slice_in_dim(query_blk, first, group_size, 0)
        grads = lax.dynamic_slice_in_dim(grad_blk, first, group_size, 0)
        listed = lax.dynamic_slice_in_dim(block_row, first, group_size, 0)
        active = lax.dynamic_slice_in_dim(live, first, group_size, 0)
        fetched = jnp.take(keyval, listed, axis=0)
        fetched_keys = fetched[..., :HD]
        fetched_values = fetched[..., HD:]
        score = (
            jnp.einsum("qad,qjcd->qajc", queries, fetched_keys, preferred_element_type=jnp.float32)
            * scale
        )
        score = jnp.where(active[:, None, :, None], score, -jnp.inf)
        top = jnp.max(score, axis=(2, 3), keepdims=True)
        expo = jnp.exp(score - top)
        prob = expo / jnp.sum(expo, axis=(2, 3), keepdims=True)
        prob_b = prob.astype(jnp.bfloat16)
        attn = jnp.einsum(
            "qajc,qjcd->qad", prob_b, fetched_values, preferred_element_type=jnp.float32
        )
        delta = jnp.sum(grads.astype(jnp.float32) * attn, axis=-1)
        dprob = jnp.einsum(
            "qad,qjcd->qajc", grads, fetched_values, preferred_element_type=jnp.float32
        )
        dscore = (prob * (dprob - delta[:, :, None, None])).astype(jnp.bfloat16)
        query_grad = (
            jnp.einsum("qajc,qjcd->qad", dscore, fetched_keys, preferred_element_type=jnp.float32)
            * scale
        )
        key_terms = (
            jnp.einsum("qajc,qad->qjcd", dscore, queries, preferred_element_type=jnp.float32)
            * scale
        )
        value_terms = jnp.einsum(
            "qajc,qad->qjcd", prob_b, grads, preferred_element_type=jnp.float32
        )
        update = jnp.concatenate((key_terms, value_terms), axis=-1)
        return (carry.at[listed].add(update), query_grad)

    firsts = jnp.arange(block_count // group_size, dtype=jnp.int32) * group_size
    keyval_grad, query_grads = lax.scan(
        one_group, jnp.zeros((block_count, BS, 2 * HD), jnp.float32), firsts
    )
    all_grads = jnp.concatenate(
        (query_grads.reshape(graph_nodes, HD), keyval_grad.reshape(graph_nodes, 2 * HD)), axis=1
    )
    all_grads = all_grads.astype(jnp.bfloat16)
    by_part = jnp.take(all_grads, order, axis=0).reshape(graph_nodes, 1, 3 * HD)
    returned = lax.all_to_all(by_part, "head", split_axis=0, concat_axis=1, tiled=True).reshape(
        local_rows, half_heads, 3, HD
    )
    full_width = w_query.shape[0]

    def term_for(weight, member):
        shaped_weight = weight.reshape(full_width, half_heads, HD)
        piece = returned[:, :, member]
        return jnp.einsum("rhd,ehd->re", piece, shaped_weight, preferred_element_type=jnp.float32)

    total = lax.psum_scatter(term_for(w_query, 0), "tensor", scatter_dimension=0, tiled=True)
    total = total + lax.psum_scatter(term_for(w_key, 1), "tensor", scatter_dimension=0, tiled=True)
    total = total + lax.psum_scatter(
        term_for(w_value, 2), "tensor", scatter_dimension=0, tiled=True
    )
    return total.astype(jnp.bfloat16)


def solution(mesh):
    return jax.shard_map(
        on_device,
        mesh=mesh,
        in_specs=(
            P(("groups", "head"), "tensor"),
            P(("groups", "head"), "tensor"),
            P(("groups", "head"), "tensor"),
            P(("groups", "head"), "tensor"),
            P("tensor", None),
            P(None, "tensor"),
            P(None, "tensor"),
            P(None, "tensor"),
            P("groups", None),
            P("groups", None, None),
            P("groups", None),
        ),
        out_specs=P(("groups", "head", "tensor"), None),
        check_vma=False,
    )
```

profile of v0, /device:TPU:0, one launch (start us, length us, event | category | flops | bytes accessed | tf_op | source)
XLA Modules:
  0.0 487.7 jit_solution(12786083107851520610)
XLA Ops:
  10.0 10.7 %all-gather.2.cloned.1.call-done = bf16[512,1024]{1,0:T(8,128)(2,1)} async-done(((bf16[512,512]{1,0:T(8,128)(2,1)}), bf16[512,1024]{1,0:T(8,128)(2,1)}) %all-gather.2.cloned.1.call-update) | async-done | bytes 1048592 | tf_op jit(solution)/shard_map/all_gather | solution.py:22
  24.5 5.9 %all-to-all-start = ((bf16[512,8,256]{0,2,1:T(8,128)(2,1)}), bf16[512,8,256]{0,2,1:T(8,128)(2,1)S(1)}, u32[]{:S(2)}, u32[]{:S(2)}) async-start(bf16[512,8,256]{0,2,1:T(8,128)(2,1)} %bitcast.136), calls=%async_computation | async-start | bytes 4194304 | tf_op jit(solution)/shard_map/all_to_all | solution.py:32
  30.5 15.7 %scatter_custom_fusion.1 = s32[4096]{0:T(1024)S(1)} fusion(s32[4096]{0:T(1024)S(1)} %bitcast.150, s32[4096]{0:T(1024)S(1)} %iota.11, s32[]{:T(128)} %constant.74.clone.1), kind=kCustom, calls=%fused_computation.62 | custom fusion | bytes 16388 | tf_op jit(solution)/shard_map/scatter | solution.py:39
  46.4 32.7 %all-to-all-done = bf16[512,8,256]{0,2,1:T(8,128)(2,1)S(1)} async-done(((bf16[512,8,256]{0,2,1:T(8,128)(2,1)}), bf16[512,8,256]{0,2,1:T(8,128)(2,1)S(1)}, u32[]{:S(2)}, u32[]{:S(2)}) %all-to-all-start) | async-done | bytes 2097184 | tf_op jit(solution)/shard_map/all_to_all | solution.py:32
  80.4 2.8 copy.144
  83.3 3.3 reshape.170
  86.5 30.7 %gather_fusion.1 = bf16[4096,4,64]{2,1,0:T(4,128)(2,1)} fusion(bf16[4096,4,64]{2,1,0:T(4,128)(2,1)} %reshape.170, s32[4096]{0:T(1024)S(1)} %fusion.24), kind=kCustom, calls=%fused_computation.1 | custom fusion | bytes 4210688 | tf_op jit(solution)/shard_map/jit(_take)/gather | solution.py:41
  117.2 4.8 copy.145
  125.9 248.2 %while.12 = (s32[]{:T(128)}, f32[32,128,128]{2,1,0:T(8,128)}, bf16[8,4,128,64]{2,3,1,0:T(8,128)(2,1)}, s32[8]{0:T(128)S(1)}, s32[32,12]{1,0:T(8,128)S(1)}, /*ind...) while((s32[]{:T(128)}, f32[32,128,128]{2,1,0:T(8,128)}, ...), condition=%wide.region_6.7_spmd, body=%wide.region_1.0_spmd.sunk | while | flops 625737472 | bytes 73627488 | solution.py:89
  134.9 2.7 multiply_convert_fusion.2
  142.7 2.4 copy.192
  145.1 9.1 %scatter_fusion = f32[32,128,128]{2,1,0:T(8,128)} fusion(f32[32,128,128]{2,1,0:T(8,128)} %get-tuple-element.203, s32[48]{0:T(128)S(1)} %reshape.184, f32[48,128,128]{2,1,0:T(8,128)S(1)} %copy.192), kind=kCustom, calls=%fused_computation.3.clone.1 | custom fusion | flops 786432 | bytes 9437376 | tf_op jit(solution)/shard_map/while/body/eval_jaxpr/scatter-add | solution.py:86
  154.2 2.8 fusion.62
  166.0 2.7 multiply_convert_fusion.2
  173.8 2.4 copy.192
  176.2 9.0 %scatter_fusion = f32[32,128,128]{2,1,0:T(8,128)} fusion(f32[32,128,128]{2,1,0:T(8,128)} %get-tuple-element.203, s32[48]{0:T(128)S(1)} %reshape.184, f32[48,128,128]{2,1,0:T(8,128)S(1)} %copy.192), kind=kCustom, calls=%fused_computation.3.clone.1 | custom fusion | flops 786432 | bytes 9437376 | tf_op jit(solution)/shard_map/while/body/eval_jaxpr/scatter-add | solution.py:86
  185.3 2.8 fusion.62
  197.1 2.7 multiply_convert_fusion.2
  204.9 2.4 copy.192
  207.3 9.0 %scatter_fusion = f32[32,128,128]{2,1,0:T(8,128)} fusion(f32[32,128,128]{2,1,0:T(8,128)} %get-tuple-element.203, s32[48]{0:T(128)S(1)} %reshape.184, f32[48,128,128]{2,1,0:T(8,128)S(1)} %copy.192), kind=kCustom, calls=%fused_computation.3.clone.1 | custom fusion | flops 786432 | bytes 9437376 | tf_op jit(solution)/shard_map/while/body/eval_jaxpr/scatter-add | solution.py:86
  216.3 2.8 fusion.62
  228.1 2.7 multiply_convert_fusion.2
  235.9 2.4 copy.192
  238.3 9.0 %scatter_fusion = f32[32,128,128]{2,1,0:T(8,128)} fusion(f32[32,128,128]{2,1,0:T(8,128)} %get-tuple-element.203, s32[48]{0:T(128)S(1)} %reshape.184, f32[48,128,128]{2,1,0:T(8,128)S(1)} %copy.192), kind=kCustom, calls=%fused_computation.3.clone.1 | custom fusion | flops 786432 | bytes 9437376 | tf_op jit(solution)/shard_map/while/body/eval_jaxpr/scatter-add | solution.py:86
  247.3 2.8 fusion.62
  259.1 2.7 multiply_convert_fusion.2
  266.9 2.4 copy.192
  269.3 9.0 %scatter_fusion = f32[32,128,128]{2,1,0:T(8,128)} fusion(f32[32,128,128]{2,1,0:T(8,128)} %get-tuple-element.203, s32[48]{0:T(128)S(1)} %reshape.184, f32[48,128,128]{2,1,0:T(8,128)S(1)} %copy.192), kind=kCustom, calls=%fused_computation.3.clone.1 | custom fusion | flops 786432 | bytes 9437376 | tf_op jit(solution)/shard_map/while/body/eval_jaxpr/scatter-add | solution.py:86
  278.3 2.8 fusion.62
  290.1 2.7 multiply_convert_fusion.2
  298.0 2.4 copy.192
  300.3 9.0 %scatter_fusion = f32[32,128,128]{2,1,0:T(8,128)} fusion(f32[32,128,128]{2,1,0:T(8,128)} %get-tuple-element.203, s32[48]{0:T(128)S(1)} %reshape.184, f32[48,128,128]{2,1,0:T(8,128)S(1)} %copy.192), kind=kCustom, calls=%fused_computation.3.clone.1 | custom fusion | flops 786432 | bytes 9437376 | tf_op jit(solution)/shard_map/while/body/eval_jaxpr/scatter-add | solution.py:86
  309.4 2.8 fusion.62
  321.1 2.7 multiply_convert_fusion.2
  328.9 2.4 copy.192
  331.3 9.0 %scatter_fusion = f32[32,128,128]{2,1,0:T(8,128)} fusion(f32[32,128,128]{2,1,0:T(8,128)} %get-tuple-element.203, s32[48]{0:T(128)S(1)} %reshape.184, f32[48,128,128]{2,1,0:T(8,128)S(1)} %copy.192), kind=kCustom, calls=%fused_computation.3.clone.1 | custom fusion | flops 786432 | bytes 9437376 | tf_op jit(solution)/shard_map/while/body/eval_jaxpr/scatter-add | solution.py:86
  340.3 2.8 fusion.62
  352.1 2.7 multiply_convert_fusion.2
  362.3 9.0 %scatter_fusion = f32[32,128,128]{2,1,0:T(8,128)} fusion(f32[32,128,128]{2,1,0:T(8,128)} %get-tuple-element.203, s32[48]{0:T(128)S(1)} %reshape.184, f32[48,128,128]{2,1,0:T(8,128)S(1)} %copy.192), kind=kCustom, calls=%fused_computation.3.clone.1 | custom fusion | flops 786432 | bytes 9437376 | tf_op jit(solution)/shard_map/while/body/eval_jaxpr/scatter-add | solution.py:86
  371.3 2.8 fusion.62
  378.3 16.9 %gather_fusion.2 = bf16[4096,192]{1,0:T(8,128)(2,1)} fusion(bf16[4096,192]{1,0:T(8,128)(2,1)S(1)} %pad_maximum_fusion.2, s32[4096]{0:T(1024)S(1)} %broadcast_clamp_fusion), kind=kCustom, calls=%fused_computation.2 | custom fusion | bytes 3162112 | tf_op jit(solution)/shard_map/jit(_take)/gather | solution.py:96
  397.7 3.1 reduce
  400.8 6.7 %reshape.173 = bf16[8,2,49152]{2,1,0:T(2,128)(2,1)} reshape(bf16[4096,192]{1,0:T(8,128)(2,1)} %reduce) | data formatting | bytes 3145728
  407.5 3.8 all-to-all-start.1
  416.3 32.2 %all-to-all-done.1 = bf16[8,2,49152]{2,1,0:T(2,128)(2,1)S(1)} async-done(((bf16[8,2,49152]{2,1,0:T(2,128)(2,1)}), bf16[8,2,49152]{2,1,0:T(2,128)(2,1)S(1)}, u32[]{:S(2)}, u32[]{:S(2)}) %all-to-all-start.1) | async-done | bytes 1572896 | tf_op jit(solution)/shard_map/all_to_all | solution.py:97
  448.4 4.9 %reshape.174 = bf16[4096,1,192]{2,1,0:T(2,128)(2,1)} reshape(bf16[8,2,49152]{2,1,0:T(2,128)(2,1)S(1)} %all-to-all-done.1) | data formatting | bytes 3145728
  453.3 9.9 %copy.127 = bf16[4096,1,192]{0,2,1:T(8,128)(2,1)S(1)} copy(bf16[4096,1,192]{2,1,0:T(2,128)(2,1)} %reshape.174) | data formatting | bytes 3145728 | tf_op jit(solution)/shard_map/all_to_all | solution.py:97
  469.7 9.0 %reduce-scatter.2.cloned.1.call-done = f32[256,1024]{1,0:T(8,128)} async-done(((f32[512,1024]{1,0:T(8,128)}), f32[256,1024]{1,0:T(8,128)}) %reduce-scatter.2.cloned.1.call-update) | async-done | bytes 1048592 | tf_op jit(solution)/shard_map/reduce_scatter | solution.py:107
  (224 shorter events, 132.4 us)
Async XLA Ops:
  6.5 14.1 %copy-start = (bf16[512,1024]{1,0:T(8,128)(2,1)S(1)}, bf16[512,1024]{1,0:T(8,128)(2,1)}, u32[]{:S(2)}) copy-start(bf16[512,1024]{1,0:T(8,128)(2,1)} %param.17) | copy-start | bytes 3145732
  6.5 3.2 copy-start.11
  6.5 14.1 %all-gather.2.cloned.1.call-start = ((), (), s32[]{:S(2)}) async-start(), calls=%async_computation.3 | async-start | bytes 1572864 | tf_op jit(solution)/shard_map/all_gather | solution.py:22
  24.5 5.9 %copy-start.13 = (s32[1,32,12]{1,0,2:T(1,128)S(1)}, s32[1,32,12]{1,0,2:T(1,128)}, u32[]{:S(2)}) copy-start(s32[1,32,12]{1,0,2:T(1,128)} %param.22) | copy-start | bytes 4612
  24.5 6.0 %copy-start.12 = (s32[1,4096]{1,0:T(1,128)S(1)}, s32[1,4096]{1,0:T(1,128)}, u32[]{:S(2)}) copy-start(s32[1,4096]{1,0:T(1,128)} %param.21) | copy-start | bytes 49156
  24.5 21.8 %copy-start.14 = (s32[1,32]{1,0:T(1,128)S(1)}, s32[1,32]{1,0:T(1,128)}, u32[]{:S(2)}) copy-start(s32[1,32]{1,0:T(1,128)} %param.23) | copy-start | bytes 388
  24.5 54.6 %all-to-all-start = ((bf16[512,8,256]{0,2,1:T(8,128)(2,1)}), bf16[512,8,256]{0,2,1:T(8,128)(2,1)S(1)}, u32[]{:S(2)}, u32[]{:S(2)}) async-start(bf16[512,8,256]{0,2,1:T(8,128)(2,1)} %bitcast.136), calls=%async_computation | async-start | bytes 4194304 | tf_op jit(solution)/shard_map/all_to_all | solution.py:32
  79.1 1.3 copy-start.5
  125.9 2.7 copy-start.3
  130.6 4.3 copy-start.2
  154.2 2.8 copy-start.4
  157.0 2.7 copy-start.3
  161.7 4.3 copy-start.2
  185.3 2.8 copy-start.4
  188.1 2.7 copy-start.3
  192.8 4.3 copy-start.2
  216.3 2.8 copy-start.4
  219.1 2.7 copy-start.3
  223.8 4.3 copy-start.2
  247.3 2.8 copy-start.4
  250.1 2.7 copy-start.3
  254.8 4.3 copy-start.2
  278.3 2.8 copy-start.4
  281.1 2.7 copy-start.3
  285.8 4.3 copy-start.2
  309.4 2.8 copy-start.4
  312.2 2.7 copy-start.3
  316.9 4.2 copy-start.2
  340.3 2.8 copy-start.4
  343.1 2.7 copy-start.3
  347.9 4.2 copy-start.2
  371.3 2.8 copy-start.4
  407.5 3.8 copy-start.6
  407.5 41.0 %all-to-all-start.1 = ((bf16[8,2,49152]{2,1,0:T(2,128)(2,1)}), bf16[8,2,49152]{2,1,0:T(2,128)(2,1)S(1)}, u32[]{:S(2)}, u32[]{:S(2)}) async-start(bf16[8,2,49152]{2,1,0:T(2,128)(2,1)} %reshape.173), calls=%async_computation.1 | async-start | bytes 3145728 | tf_op jit(solution)/shard_map/all_to_all | solution.py:97
  411.3 67.5 %reduce-scatter.2.cloned.1.call-start = ((), (), s32[]{:S(2)}) async-start(), calls=%async_computation.4 | async-start | bytes 3145728 | tf_op jit(solution)/shard_map/reduce_scatter | solution.py:107
  412.6 2.4 copy-start.7
  463.9 1.2 copy-start.10
  465.1 1.2 copy-start.9
  466.3 1.2 copy-start.8
  467.6 13.3 %copy-start.1 = (bf16[512,1024]{1,0:T(8,128)(2,1)S(1)}, bf16[512,1024]{1,0:T(8,128)(2,1)}, u32[]{:S(2)}) copy-start(bf16[512,1024]{1,0:T(8,128)(2,1)} %param.17) | copy-start | bytes 3145732
Sparse Core Ops, SparseCore 0:
  8.9 11.7 all-gather.1
  469.8 8.8 reduce-scatter.1
where the time goes:
time: 491 us; the launch traced here: 488 us
  local copies, waits for them, and re-layouts  166 us (34%)
  other arithmetic  107 us (22%)
  matrix products  90.5 us (18%)
  waiting for transfers between devices  85.3 us (17%)
  loops' own time  15.5 us (3%)
  between operations  13.6 us (3%)
  starting transfers between devices  9.72 us (2%)
    scatter-add x8, other arithmetic, one_group(): return (carry.at[listed].add(update), query_grad)  72.1 us
    gather x2, local copies, waits for them, and re-layouts, on_device(): by_node = jnp.take(arrived, inverse, axis=0).reshape(block_count, BS, 4, HD)  35.5 us
    all_to_all x1, waiting for transfers between devices, on_device(): lax.all_to_all(packed, 'head', split_axis=1, concat_axis=0, tiled=True)  32.7 us
    all_to_all x1, waiting for transfers between devices, on_device(): lax.all_to_all(by_part, 'head', split_axis=0, concat_axis=1, tiled=True)  32.2 us
    unnamed x34, local copies, waits for them, and re-layouts  23.4 us
    dot_general x8, matrix products, one_group(): jnp.einsum('qajc,qjcd->qad', dscore, fetched_keys, preferred_element_type...  22.4 us
    dot_general x8, matrix products, one_group(): jnp.einsum('qad,qjcd->qajc', grads, fetched_values, preferred_element_typ...  22 us
    concatenate x8, local copies, waits for them, and re-layouts, one_group(): update = jnp.concatenate((key_terms, value_terms), axis=-1)  19 us
  transfers between devices with their start and end apart: 4, of which 4 were waited for; matrix products, arithmetic and copies ran while one was open for 5% of the time, Pallas kernels for 0%

commit v1 on v0

--- a/solution.py
+++ b/solution.py
@@ -6,6 +6,22 @@
 HD = 64
 BS = 128
 KB = 12
+
+
+def swapped_with_each(x, axis, split, join):
+    ways, here = (lax.axis_size(axis), lax.axis_index(axis))
+    width = x.shape[split] // ways
+    shape = list(x.shape)
+    shape[split] = width
+    height = shape[join]
+    shape[join] = height * ways
+    full = jnp.zeros(shape, x.dtype)
+    for mask in range(ways):
+        part = lax.dynamic_slice_in_dim(x, (here ^ mask) * width, width, axis=split)
+        if mask:
+            part = lax.ppermute(part, axis, [(d, d ^ mask) for d in range(ways)])
+        full = lax.dynamic_update_slice_in_dim(full, part, (here ^ mask) * height, axis=join)
+    return full
 
 
 def on_device(
@@ -94,9 +110,7 @@
     )
     all_grads = all_grads.astype(jnp.bfloat16)
     by_part = jnp.take(all_grads, order, axis=0).reshape(graph_nodes, 1, 3 * HD)
-    returned = lax.all_to_all(by_part, "head", split_axis=0, concat_axis=1, tiled=True).reshape(
-        local_rows, half_heads, 3, HD
-    )
+    returned = swapped_with_each(by_part, "head", 0, 1).reshape(local_rows, half_heads, 3, HD)
     full_width = w_query.shape[0]
 
     def term_for(weight, member):

time: 491 us -> 468 us (0.953)
  local copies, waits for them, and re-layouts: 166 us -> 149 us
  waiting for transfers between devices: 85.3 us -> 73.3 us
  starting transfers between devices: 9.72 us -> 16 us
    all_to_all x1 -> x0, waiting for transfers between devices: 32.2 us -> none  [on_device(): lax.all_to_all(by_part, 'head', split_axis=0, concat_axis=1, tiled=True)]
    ppermute x0 -> x7, waiting for transfers between devices: none -> 19.9 us  [swapped_with_each(): part = lax.ppermute(part, axis, [(d, d ^ mask) for d in range(ways)])]
    unnamed x34 -> x29, local copies, waits for them, and re-layouts: 23.4 us -> 9.69 us
    ppermute x0 -> x7, starting transfers between devices: none -> 10 us  [swapped_with_each(): part = lax.ppermute(part, axis, [(d, d ^ mask) for d in range(ways)])]
    all_to_all x1 -> x0, local copies, waits for them, and re-layouts: 9.89 us -> none  [on_device(): lax.all_to_all(by_part, 'head', split_axis=0, concat_axis=1, tiled=True)]
    reduce_scatter x1, waiting for transfers between devices: 9.05 us -> 14.5 us  [on_device(): lax.psum_scatter(term_for(w_query, 0), 'tensor', scatter_dimension=0, til...]
    all_to_all x1, waiting for transfers between devices: 32.7 us -> 27.5 us  [on_device(): lax.all_to_all(packed, 'head', split_axis=1, concat_axis=0, tiled=True)]
  transfers between devices with their start and end apart: 4 -> 10, of which waited for: 4 -> 7; matrix products, arithmetic and copies ran while one was open for 5% -> 6% of each run, Pallas kernels for 0% -> 0%
where the time goes in v1:
time: 468 us; the launch traced here: 464 us
  local copies, waits for them, and re-layouts  149 us (32%)
  other arithmetic  104 us (22%)
  matrix products  91.4 us (20%)
  waiting for transfers between devices  73.3 us (16%)
  loops' own time  17.1 us (4%)
  starting transfers between devices  16 us (3%)
  between operations  13.9 us (3%)
    scatter-add x8, other arithmetic, one_group(): return (carry.at[listed].add(update), query_grad)  72.6 us
    gather x2, local copies, waits for them, and re-layouts, on_device(): by_node = jnp.take(arrived, inverse, axis=0).reshape(block_count, BS, 4, HD)  35.7 us
    all_to_all x1, waiting for transfers between devices, on_device(): lax.all_to_all(packed, 'head', split_axis=1, concat_axis=0, tiled=True)  27.5 us
    dot_general x8, matrix products, one_group(): jnp.einsum('qajc,qjcd->qad', dscore, fetched_keys, preferred_element_type...  22.4 us
    dot_general x8, matrix products, one_group(): jnp.einsum('qad,qjcd->qajc', grads, fetched_values, preferred_element_typ...  21.6 us
    ppermute x7, waiting for transfers between devices, swapped_with_each(): part = lax.ppermute(part, axis, [(d, d ^ mask) for d in range(ways)])  19.9 us
    concatenate x8, local copies, waits for them, and re-layouts, one_group(): update = jnp.concatenate((key_terms, value_terms), axis=-1)  19 us
    another operation x1, loops' own time, on_device(): lax.scan(one_group, jnp.zeros((block_count, BS, 2 * HD), jnp.float32), fi...  17.1 us
  transfers between devices with their start and end apart: 10, of which 7 were waited for; matrix products, arithmetic and copies ran while one was open for 6% of the time, Pallas kernels for 0%

profile of v1, /device:TPU:0, one launch (start us, length us, event | category | flops | bytes accessed | tf_op | source)
XLA Modules:
  0.0 464.4 jit_solution(14963507805512819056)
XLA Ops:
  10.0 10.7 %all-gather.2.cloned.1.call-done = bf16[512,1024]{1,0:T(8,128)(2,1)} async-done(((bf16[512,512]{1,0:T(8,128)(2,1)}), bf16[512,1024]{1,0:T(8,128)(2,1)}) %all-gather.2.cloned.1.call-update) | async-done | bytes 1048592 | tf_op jit(solution)/shard_map/all_gather | solution.py:38
  24.5 5.9 %all-to-all-start = ((bf16[512,8,256]{0,2,1:T(8,128)(2,1)}), bf16[512,8,256]{0,2,1:T(8,128)(2,1)S(1)}, u32[]{:S(2)}, u32[]{:S(2)}) async-start(bf16[512,8,256]{0,2,1:T(8,128)(2,1)} %bitcast.137), calls=%async_computation | async-start | bytes 4194304 | tf_op jit(solution)/shard_map/all_to_all | solution.py:48
  32.0 2.4 copy.82
  35.7 15.7 %scatter_custom_fusion.1 = s32[4096]{0:T(1024)S(1)} fusion(s32[4096]{0:T(1024)S(1)} %bitcast.158, s32[4096]{0:T(1024)S(1)} %iota.11, s32[]{:T(128)} %constant.57.clone.1), kind=kCustom, calls=%fused_computation.63 | custom fusion | bytes 16388 | tf_op jit(solution)/shard_map/scatter | solution.py:55
  51.6 27.5 %all-to-all-done = bf16[512,8,256]{0,2,1:T(8,128)(2,1)S(1)} async-done(((bf16[512,8,256]{0,2,1:T(8,128)(2,1)}), bf16[512,8,256]{0,2,1:T(8,128)(2,1)S(1)}, u32[]{:S(2)}, u32[]{:S(2)}) %all-to-all-start) | async-done | bytes 2097184 | tf_op jit(solution)/shard_map/all_to_all | solution.py:48
  80.4 2.8 copy.94
  83.3 3.2 reshape.154
  86.5 30.9 %gather_fusion.1 = bf16[4096,4,64]{2,1,0:T(4,128)(2,1)} fusion(bf16[4096,4,64]{2,1,0:T(4,128)(2,1)} %reshape.154, s32[4096]{0:T(1024)S(1)} %fusion.24), kind=kCustom, calls=%fused_computation.1 | custom fusion | bytes 4210688 | tf_op jit(solution)/shard_map/jit(_take)/gather | solution.py:57
  117.4 4.8 %copy.95 = bf16[32,128,4,64]{1,0,3,2:T(8,128)(2,1)S(1)} copy(bf16[32,128,4,64]{3,2,1,0:T(4,128)(2,1)} %bitcast.135) | data formatting | bytes 4194304 | tf_op jit(solution)/shard_map/jit(_take)/gather | solution.py:57
  126.2 250.3 %while.12 = (s32[]{:T(128)}, f32[32,128,128]{2,1,0:T(8,128)}, bf16[8,4,128,64]{2,3,1,0:T(8,128)(2,1)}, s32[8]{0:T(128)S(1)}, s32[32,12]{1,0:T(8,128)S(1)}, /*ind...) while((s32[]{:T(128)}, f32[32,128,128]{2,1,0:T(8,128)}, ...), condition=%wide.region_6.7_spmd, body=%wide.region_1.0_spmd.sunk | while | flops 625737472 | bytes 73627488 | solution.py:105
  135.5 2.7 multiply_convert_fusion.2
  143.2 2.4 copy.131
  145.6 9.1 %scatter_fusion = f32[32,128,128]{2,1,0:T(8,128)} fusion(f32[32,128,128]{2,1,0:T(8,128)} %get-tuple-element.190, s32[48]{0:T(128)S(1)} %reshape.166, f32[48,128,128]{2,1,0:T(8,128)S(1)} %copy.131), kind=kCustom, calls=%fused_computation.3.clone.1 | custom fusion | flops 786432 | bytes 9437376 | tf_op jit(solution)/shard_map/while/body/eval_jaxpr/scatter-add | solution.py:102
  154.7 2.8 fusion.61
  166.8 2.7 multiply_convert_fusion.2
  174.5 2.4 copy.131
  176.9 9.1 %scatter_fusion = f32[32,128,128]{2,1,0:T(8,128)} fusion(f32[32,128,128]{2,1,0:T(8,128)} %get-tuple-element.190, s32[48]{0:T(128)S(1)} %reshape.166, f32[48,128,128]{2,1,0:T(8,128)S(1)} %copy.131), kind=kCustom, calls=%fused_computation.3.clone.1 | custom fusion | flops 786432 | bytes 9437376 | tf_op jit(solution)/shard_map/while/body/eval_jaxpr/scatter-add | solution.py:102
  186.0 2.8 fusion.61
  198.1 2.7 multiply_convert_fusion.2
  205.9 2.4 copy.131
  208.3 9.1 %scatter_fusion = f32[32,128,128]{2,1,0:T(8,128)} fusion(f32[32,128,128]{2,1,0:T(8,128)} %get-tuple-element.190, s32[48]{0:T(128)S(1)} %reshape.166, f32[48,128,128]{2,1,0:T(8,128)S(1)} %copy.131), kind=kCustom, calls=%fused_computation.3.clone.1 | custom fusion | flops 786432 | bytes 9437376 | tf_op jit(solution)/shard_map/while/body/eval_jaxpr/scatter-add | solution.py:102
  217.4 2.8 fusion.61
  229.4 2.7 multiply_convert_fusion.2
  237.2 2.4 copy.131
  239.6 9.0 %scatter_fusion = f32[32,128,128]{2,1,0:T(8,128)} fusion(f32[32,128,128]{2,1,0:T(8,128)} %get-tuple-element.190, s32[48]{0:T(128)S(1)} %reshape.166, f32[48,128,128]{2,1,0:T(8,128)S(1)} %copy.131), kind=kCustom, calls=%fused_computation.3.clone.1 | custom fusion | flops 786432 | bytes 9437376 | tf_op jit(solution)/shard_map/while/body/eval_jaxpr/scatter-add | solution.py:102
  248.6 2.8 fusion.61
  260.7 2.7 multiply_convert_fusion.2
  268.5 2.4 copy.131
  270.8 9.1 %scatter_fusion = f32[32,128,128]{2,1,0:T(8,128)} fusion(f32[32,128,128]{2,1,0:T(8,128)} %get-tuple-element.190, s32[48]{0:T(128)S(1)} %reshape.166, f32[48,128,128]{2,1,0:T(8,128)S(1)} %copy.131), kind=kCustom, calls=%fused_computation.3.clone.1 | custom fusion | flops 786432 | bytes 9437376 | tf_op jit(solution)/shard_map/while/body/eval_jaxpr/scatter-add | solution.py:102
  279.9 2.8 fusion.61
  292.0 2.7 multiply_convert_fusion.2
  299.8 2.4 copy.131
  302.2 9.1 %scatter_fusion = f32[32,128,128]{2,1,0:T(8,128)} fusion(f32[32,128,128]{2,1,0:T(8,128)} %get-tuple-element.190, s32[48]{0:T(128)S(1)} %reshape.166, f32[48,128,128]{2,1,0:T(8,128)S(1)} %copy.131), kind=kCustom, calls=%fused_computation.3.clone.1 | custom fusion | flops 786432 | bytes 9437376 | tf_op jit(solution)/shard_map/while/body/eval_jaxpr/scatter-add | solution.py:102
  311.2 2.8 fusion.61
  323.2 2.7 multiply_convert_fusion.2
  331.0 2.4 copy.131
  333.4 9.1 %scatter_fusion = f32[32,128,128]{2,1,0:T(8,128)} fusion(f32[32,128,128]{2,1,0:T(8,128)} %get-tuple-element.190, s32[48]{0:T(128)S(1)} %reshape.166, f32[48,128,128]{2,1,0:T(8,128)S(1)} %copy.131), kind=kCustom, calls=%fused_computation.3.clone.1 | custom fusion | flops 786432 | bytes 9437376 | tf_op jit(solution)/shard_map/while/body/eval_jaxpr/scatter-add | solution.py:102
  342.5 2.8 fusion.61
  354.5 2.7 multiply_convert_fusion.2
  362.3 2.4 copy.131
  364.6 9.1 %scatter_fusion = f32[32,128,128]{2,1,0:T(8,128)} fusion(f32[32,128,128]{2,1,0:T(8,128)} %get-tuple-element.190, s32[48]{0:T(128)S(1)} %reshape.166, f32[48,128,128]{2,1,0:T(8,128)S(1)} %copy.131), kind=kCustom, calls=%fused_computation.3.clone.1 | custom fusion | flops 786432 | bytes 9437376 | tf_op jit(solution)/shard_map/while/body/eval_jaxpr/scatter-add | solution.py:102
  373.7 2.8 fusion.61
  380.7 17.0 %gather_fusion.2 = bf16[4096,192]{1,0:T(8,128)(2,1)} fusion(bf16[4096,192]{1,0:T(8,128)(2,1)S(1)} %pad_maximum_fusion.2, s32[4096]{0:T(1024)S(1)} %broadcast_clamp_fusion), kind=kCustom, calls=%fused_computation.2 | custom fusion | bytes 3162112 | tf_op jit(solution)/shard_map/jit(_take)/gather | solution.py:112
  405.8 3.1 collective-permute-start.4
  411.8 4.6 collective-permute-done.1
  419.4 11.1 %collective-permute-done.3 = bf16[512,1,192]{0,2,1:T(8,128)(2,1)} collective-permute-done((bf16[512,1,192]{0,2,1:T(8,128)(2,1)S(1)}, bf16[512,1,192]{0,2,1:T(8,128)(2,1)}, u32[]{:S(2)}, u32[]{:S(2)}) %collective-permute-start.3) | collective-permute-done | bytes 196640 | tf_op jit(solution)/shard_map/ppermute | solution.py:22
  431.4 4.1 collective-permute-done.4
  441.0 14.5 %reduce-scatter.2.cloned.1.call-done = f32[256,1024]{1,0:T(8,128)} async-done(((f32[512,1024]{1,0:T(8,128)}), f32[256,1024]{1,0:T(8,128)}) %reduce-scatter.2.cloned.1.call-update) | async-done | bytes 1048592 | tf_op jit(solution)/shard_map/reduce_scatter | solution.py:121
  (245 shorter events, 139.6 us)
Async XLA Ops:
  6.5 14.1 %copy-start = (bf16[512,1024]{1,0:T(8,128)(2,1)S(1)}, bf16[512,1024]{1,0:T(8,128)(2,1)}, u32[]{:S(2)}) copy-start(bf16[512,1024]{1,0:T(8,128)(2,1)} %param.17) | copy-start | bytes 3145732
  6.5 3.2 copy-start.10
  6.5 14.1 %all-gather.2.cloned.1.call-start = ((), (), s32[]{:S(2)}) async-start(), calls=%async_computation.2 | async-start | bytes 1572864 | tf_op jit(solution)/shard_map/all_gather | solution.py:38
  24.5 6.1 %copy-start.12 = (s32[1,32,12]{1,0,2:T(1,128)S(1)}, s32[1,32,12]{1,0,2:T(1,128)}, u32[]{:S(2)}) copy-start(s32[1,32,12]{1,0,2:T(1,128)} %param.22) | copy-start | bytes 4612
  24.5 6.2 %copy-start.6 = (bf16[1024,512]{1,0:T(8,128)(2,1)S(1)}, bf16[1024,512]{1,0:T(8,128)(2,1)}, u32[]{:S(2)}) copy-start(bf16[1024,512]{1,0:T(8,128)(2,1)} %param.18) | copy-start | bytes 3145732
  24.5 54.6 %all-to-all-start = ((bf16[512,8,256]{0,2,1:T(8,128)(2,1)}), bf16[512,8,256]{0,2,1:T(8,128)(2,1)S(1)}, u32[]{:S(2)}, u32[]{:S(2)}) async-start(bf16[512,8,256]{0,2,1:T(8,128)(2,1)} %bitcast.137), calls=%async_computation | async-start | bytes 4194304 | tf_op jit(solution)/shard_map/all_to_all | solution.py:48
  30.4 425.1 %reduce-scatter.2.cloned.1.call-start = ((), (), s32[]{:S(2)}) async-start(), calls=%async_computation.3 | async-start | bytes 3145728 | tf_op jit(solution)/shard_map/reduce_scatter | solution.py:121
  32.0 2.4 copy-start.7
  32.0 3.7 copy-start.11
  32.0 19.5 %copy-start.13 = (s32[1,32]{1,0:T(1,128)S(1)}, s32[1,32]{1,0:T(1,128)}, u32[]{:S(2)}) copy-start(s32[1,32]{1,0:T(1,128)} %param.23) | copy-start | bytes 388
  79.1 1.3 copy-start.5
  126.2 2.9 copy-start.3
  131.1 4.3 copy-start.2
  154.7 2.8 copy-start.4
  157.5 2.9 copy-start.3
  162.4 4.3 copy-start.2
  186.0 2.8 copy-start.4
  188.9 2.9 copy-start.3
  193.8 4.3 copy-start.2
  217.4 2.8 copy-start.4
  220.2 2.9 copy-start.3
  225.1 4.3 copy-start.2
  248.6 2.8 copy-start.4
  251.4 2.9 copy-start.3
  256.3 4.3 copy-start.2
  279.9 2.8 copy-start.4
  282.7 2.9 copy-start.3
  287.7 4.3 copy-start.2
  311.2 2.8 copy-start.4
  314.0 2.9 copy-start.3
  319.0 4.2 copy-start.2
  342.5 2.8 copy-start.4
  345.3 2.9 copy-start.3
  350.2 4.2 copy-start.2
  373.7 2.8 copy-start.4
  400.8 8.5 %collective-permute-start = (bf16[512,1,192]{0,2,1:T(8,128)(2,1)}, bf16[512,1,192]{0,2,1:T(8,128)(2,1)}, u32[]{:S(2)}, u32[]{:S(2)}) collective-permute-start(bf16[512,1,192]{0,2,1:T(8,128)(2,1)} %bitcast.33), channel_id=1, source_target_pairs={{0,2},{2,0},{4,6},{6,4},{8,10},{10,8},{12,14},{14,12},{1,3},{3,1},... | collective-permute-start | bytes 589832 | tf_op jit(solution)/shard_map/ppermute | solution.py:22
  402.4 14.0 %collective-permute-start.1 = (bf16[512,1,192]{0,2,1:T(8,128)(2,1)S(1)}, bf16[512,1,192]{0,2,1:T(8,128)(2,1)}, u32[]{:S(2)}, u32[]{:S(2)}) collective-permute-start(bf16[512,1,192]{0,2,1:T(8,128)(2,1)S(1)} %bitcast.156), channel_id=1, source_target_pairs={{0,4},{2,6},{4,0},{6,2},{8,12},{10,14},{12,8},{14,10},{1,5},{3,7},... | collective-permute-start | bytes 589832 | tf_op jit(solution)/shard_map/ppermute | solution.py:22
  402.6 15.9 %collective-permute-start.2 = (bf16[512,1,192]{0,2,1:T(8,128)(2,1)S(1)}, bf16[512,1,192]{0,2,1:T(8,128)(2,1)}, u32[]{:S(2)}, u32[]{:S(2)}) collective-permute-start(bf16[512,1,192]{0,2,1:T(8,128)(2,1)S(1)} %bitcast.154), channel_id=1, source_target_pairs={{0,6},{2,4},{4,2},{6,0},{8,14},{10,12},{12,10},{14,8},{1,7},{3,5},... | collective-permute-start | bytes 589832 | tf_op jit(solution)/shard_map/ppermute | solution.py:22
  404.8 25.7 %collective-permute-start.3 = (bf16[512,1,192]{0,2,1:T(8,128)(2,1)S(1)}, bf16[512,1,192]{0,2,1:T(8,128)(2,1)}, u32[]{:S(2)}, u32[]{:S(2)}) collective-permute-start(bf16[512,1,192]{0,2,1:T(8,128)(2,1)S(1)} %bitcast.153), channel_id=1, source_target_pairs={{0,8},{2,10},{4,12},{6,14},{8,0},{10,2},{12,4},{14,6},{1,9},{3,11}... | collective-permute-start | bytes 589832 | tf_op jit(solution)/shard_map/ppermute | solution.py:22
  405.8 29.7 %collective-permute-start.4 = (bf16[512,1,192]{0,2,1:T(8,128)(2,1)S(1)}, bf16[512,1,192]{0,2,1:T(8,128)(2,1)S(1)}, u32[]{:S(2)}, u32[]{:S(2)}) collective-permute-start(bf16[512,1,192]{0,2,1:T(8,128)(2,1)S(1)} %bitcast.152), channel_id=1, source_target_pairs={{0,10},{2,8},{4,14},{6,12},{8,2},{10,0},{12,6},{14,4},{1,11},{3,9}... | collective-permute-start | bytes 589832 | tf_op jit(solution)/shard_map/ppermute | solution.py:22
  409.3 26.2 %collective-permute-start.5 = (bf16[512,1,192]{0,2,1:T(8,128)(2,1)S(1)}, bf16[512,1,192]{0,2,1:T(8,128)(2,1)S(1)}, u32[]{:S(2)}, u32[]{:S(2)}) collective-permute-start(bf16[512,1,192]{0,2,1:T(8,128)(2,1)S(1)} %bitcast.155), channel_id=1, source_target_pairs={{0,12},{2,14},{4,8},{6,10},{8,4},{10,6},{12,0},{14,2},{1,13},{3,15... | collective-permute-start | bytes 589832 | tf_op jit(solution)/shard_map/ppermute | solution.py:22
  416.4 19.2 %collective-permute-start.6 = (bf16[512,1,192]{0,2,1:T(8,128)(2,1)S(1)}, bf16[512,1,192]{0,2,1:T(8,128)(2,1)S(1)}, u32[]{:S(2)}, u32[]{:S(2)}) collective-permute-start(bf16[512,1,192]{0,2,1:T(8,128)(2,1)S(1)} %bitcast.151), channel_id=1, source_target_pairs={{0,14},{2,12},{4,10},{6,8},{8,6},{10,4},{12,2},{14,0},{1,15},{3,13... | collective-permute-start | bytes 589832 | tf_op jit(solution)/shard_map/ppermute | solution.py:22
  435.6 2.1 copy-start.9
  437.7 1.2 copy-start.8
  438.9 18.7 %copy-start.1 = (bf16[512,1024]{1,0:T(8,128)(2,1)S(1)}, bf16[512,1024]{1,0:T(8,128)(2,1)}, u32[]{:S(2)}) copy-start(bf16[512,1024]{1,0:T(8,128)(2,1)} %param.17) | copy-start | bytes 3145732
Sparse Core Ops, SparseCore 0:
  8.9 11.7 all-gather.1
  441.1 14.2 reduce-scatter.1
